TPU v7x, 256 devices: a whole 4x4x8 slice. The times are simulated.
256 devices in a mesh: tok: 32 (over z, x), hid: 8 (over y, core).
Axes of the slice: x: 4, y: 4, z: 8, core: 2. Of those that a mesh axis runs over, the one named last changes fastest.
Arguments:
- inputs: float32 [4096, 4096], P('tok'), may hold values from -6 to 6
- cotangent: float32 [4096, 4096], P('tok'), may hold values from -6 to 6
- up_blocks: float32 [112, 4, 128, 128], P('hid', None, 'tok'), may hold values from -0.25 to 0.25
- down_blocks: float32 [112, 4, 128, 128], P('hid', None, 'tok'), may hold values from -0.25 to 0.25
- up_index: int32 [112, 4], P('hid'), may hold values from 0 to 31, all different within a row
- down_index: int32 [112, 4], P('hid'), may hold values from 0 to 31, all different within a row
- mom_up: float32 [112, 4, 128, 128], P('hid', None, 'tok'), may hold values from -6 to 6
- mom_down: float32 [112, 4, 128, 128], P('hid', None, 'tok'), may hold values from -6 to 6
Outputs:
- input_grad: float32 [4096, 4096], P('tok', 'hid')
- new_mom_up: float32 [112, 4, 128, 128], P('hid', None, 'tok')
- new_mom_down: float32 [112, 4, 128, 128], P('hid', None, 'tok')
Inputs may be any that keep to these rules, and one draw needn't show every extreme that they name: `up_index`: each row lists 4 different model blocks, and every model block appears in some row. `down_index`: each row lists 4 different model blocks, and every model block appears in some row.
All inputs are finite; a program needn't handle non-finite values.
Results may differ from a plain program's by a relative error of at most 0.0003.
Values sent between devices are 32-bit elements; how exact they have to be, the bound alone decides.
A program may use at most 64 MiB of HBM per device.

v0:
```python
import jax
import jax.numpy as jnp
from jax import lax
from jax.sharding import PartitionSpec as P


def shards(inputs, cotangent, up_blocks, down_blocks, up_index, down_index, mom_up, mom_down):
    highest = lax.Precision.HIGHEST
    row_count = inputs.shape[0]
    block = up_blocks.shape[3]
    block_count = inputs.shape[1] // block
    up_full, down_full = (
        lax.all_gather(up_blocks, "tok", axis=2, tiled=True),
        lax.all_gather(down_blocks, "tok", axis=2, tiled=True),
    )
    grad_scale = (row_count * lax.axis_size("tok")) ** (-0.5)
    x_blocks = inputs.reshape(row_count, block_count, block)
    cot_blocks = cotangent.reshape(row_count, block_count, block)
    x_sel = jnp.take(x_blocks, up_index, axis=1)
    cot_sel = jnp.take(cot_blocks, down_index, axis=1)
    pre_act = jnp.einsum("rfkd,fkdc->rfc", x_sel, up_full, precision=highest)
    sigmoid_pre = jax.nn.sigmoid(pre_act)
    activation = pre_act * sigmoid_pre
    grad_act = jnp.einsum("rfkd,fkcd->rfc", cot_sel, down_full, precision=highest)
    grad_pre = grad_act * sigmoid_pre * (1.0 + pre_act * (1.0 - sigmoid_pre))
    grad_down = grad_scale * jnp.einsum("rfc,rfkd->fkcd", activation, cot_sel, precision=highest)
    back_terms = jnp.einsum("rfc,fkdc->rfkd", grad_pre, up_full, precision=highest)
    onehot = (
        up_index[:, :, None] == jnp.arange(block_count, dtype=jnp.int32)[None, None, :]
    ).astype(jnp.float32)
    partial_value = jnp.einsum("rfkd,fkj->rjd", back_terms, onehot, precision=highest).reshape(
        row_count, -1
    )
    grad_up = grad_scale * jnp.einsum("rfkd,rfc->fkdc", x_sel, grad_pre, precision=highest)
    input_grad = lax.psum_scatter(partial_value, "hid", scatter_dimension=1, tiled=True)
    up_share, down_share = (
        lax.psum_scatter(grad_up, "tok", scatter_dimension=2, tiled=True),
        lax.psum_scatter(grad_down, "tok", scatter_dimension=2, tiled=True),
    )
    return (input_grad, 0.9 * mom_up + up_share, 0.9 * mom_down + down_share)


def solution(mesh):
    return jax.shard_map(
        shards,
        mesh=mesh,
        in_specs=(
            P("tok", None),
            P("tok", None),
            P("hid", None, "tok", None),
            P("hid", None, "tok", None),
            P("hid", None),
            P("hid", None),
            P("hid", None, "tok", None),
            P("hid", None, "tok", None),
        ),
        out_specs=(P("tok", "hid"), P("hid", None, "tok", None), P("hid", None, "tok", None)),
        check_vma=False,
    )
```

profile of v0, /device:TPU:2, one launch (start us, length us, event | category | flops | bytes accessed | tf_op | source)
XLA Modules:
  0.0 435.1 jit_solution(1202382156357738444)
XLA Ops:
  7.2 0.0 all-gather.5.cloned.1.call-start
  7.2 1.6 copy.59
  8.8 0.0 all-gather.5.cloned.1.call-update
  8.8 0.0 all-gather.3.cloned.1.call-start
  8.9 1.6 copy.51
  10.4 0.0 all-gather.3.cloned.1.call-update
  10.5 0.0 copy-start.6
  10.5 0.0 all-reduce.5.cloned.1.call-start
  10.5 3.0 copy.47
  13.5 1.9 copy.49
  15.4 0.0 copy-done.6
  15.4 0.1 copy.48
  15.5 0.1 reshape.44
  15.6 2.7 gather_fusion
  18.3 0.0 copy-start.2
  18.3 5.3 %copy.50 = f32[14,4,128,128]{2,3,1,0:T(8,128)} copy(f32[14,4,128,128]{3,2,1,0:T(8,128)} %bitcast.75) | data formatting | bytes 7340032 | tf_op jit(solution)/shard_map/jit(_take)/gather | solution.py:20
  23.6 0.1 copy.46
  23.7 0.0 copy-done.2
  23.7 0.0 copy-start.5
  23.7 1.9 copy.55
  25.6 1.9 copy.57
  27.5 0.0 copy-done.5
  27.6 0.1 copy.56
  27.7 0.1 reshape.48
  27.8 2.7 gather_fusion.1
  30.4 5.1 %copy.58 = f32[14,4,128,128]{2,3,1,0:T(8,128)} copy(f32[14,4,128,128]{3,2,1,0:T(8,128)} %bitcast.76) | data formatting | bytes 7340032 | tf_op jit(solution)/shard_map/jit(_take)/gather | solution.py:19
  35.6 0.1 copy.54
  35.7 57.8 %all-gather.5.cloned.1.call-done = f32[14,4,128,128]{3,1,0,2:T(4,128)} async-done(((f32[14,4,4,128]{3,1,0,2:T(4,128)}), f32[14,4,128,128]{3,1,0,2:T(4,128)}) %all-gather.5.cloned.1.call-update) | async-done | bytes 3670032 | tf_op jit(solution)/shard_map/all_gather | solution.py:13
  93.5 0.0 copy-start
  93.5 9.6 %fusion.39 = f32[128,14,128]{2,0,1:T(8,128)S(1)} fusion(f32[14,4,128,128]{3,1,0,2:T(4,128)} %all-gather.5.cloned.1.call-done, f32[14,4,128,128]{2,3,1,0:T(8,128)} %copy.58, pred[14,4]{1,0:T(8,128)(4,1)S(1)} %copy.54), kind=kOutput, calls=%fused_computation.33 | convolution fusion | flops 1410203648 | bytes 8257592 | tf_op jit(solution)/shard_map/rfkd,fkdc->rfc/dot_general | solution.py:21
  103.1 0.0 copy-done
  103.1 5.5 %multiply_bitcast_fusion = f32[14,4,128,128]{2,3,1,0:T(8,128)} fusion(f32[14,4,128,128]{2,3,1,0:T(8,128)S(1)} %copy-done, pred[14,4]{1,0:T(8,128)(4,1)S(1)} %copy.46, f32[128,14,128]{2,0,1:T(8,128)S(1)} %fusion.39), kind=kOutput, calls=%fused_computation.13 | convolution fusion | flops 1412038656 | bytes 8257592 | tf_op jit(solution)/shard_map/rfc,rfkd->fkcd/dot_general | solution.py:26
  108.6 65.5 %all-gather.3.cloned.1.call-done = f32[14,4,128,128]{3,1,0,2:T(4,128)} async-done(((f32[14,4,4,128]{3,1,0,2:T(4,128)}), f32[14,4,128,128]{3,1,0,2:T(4,128)}) %all-gather.3.cloned.1.call-update) | async-done | bytes 3670032 | tf_op jit(solution)/shard_map/all_gather | solution.py:14
  174.0 0.0 copy-start.1
  174.0 9.8 %fusion.54 = f32[128,14,128,1]{2,0,3,1:T(8,128)S(1)} fusion(f32[14,4,128,128]{3,1,0,2:T(4,128)} %all-gather.3.cloned.1.call-done, f32[14,4,128,128]{2,3,1,0:T(8,128)} %copy.50, pred[14,4]{1,0:T(8,128)(4,1)S(1)} %copy.46, f32[128,14,128]{2,0,1:T(8,128)S(1)} %fusion.39), kind=kOutput, calls=%fused_computation.36 | convolution fusion | flops 1412038656 | bytes 9175096 | tf_op jit(solution)/shard_map/rfkd,fkcd->rfc/dot_general | solution.py:24
  183.8 0.0 copy-done.1
  183.8 5.3 %fusion.20 = f32[14,4,128,128]{3,2,1,0:T(8,128)} fusion(f32[128,14,128,1]{2,0,3,1:T(8,128)S(1)} %fusion.54, f32[14,4,128,128]{2,3,1,0:T(8,128)S(1)} %copy-done.1, pred[14,4]{1,0:T(8,128)(4,1)S(1)} %copy.54), kind=kOutput, calls=%fused_computation.22 | convolution fusion | flops 1411121152 | bytes 8257592 | tf_op jit(solution)/shard_map/rfkd,rfc->fkdc/dot_general | solution.py:34
  189.1 5.1 %copy.64 = f32[14,4,128,128]{3,2,1,0:T(8,128)} copy(f32[14,4,128,128]{2,3,1,0:T(8,128)} %multiply_bitcast_fusion) | data formatting | bytes 7340032 | tf_op jit(solution)/shard_map/mul | solution.py:26
  194.3 0.0 all-reduce.5.cloned.1.call-update
  194.3 0.3 reduce-scatter.4.cloned.1.call-start
  194.6 6.0 %fusion.23 = f32[128,14,4,128]{3,0,2,1:T(8,128)S(1)} fusion(f32[128,14,128,1]{2,0,3,1:T(8,128)S(1)} %fusion.54, f32[14,4,128,128]{3,1,0,2:T(4,128)} %all-gather.5.cloned.1.call-done), kind=kOutput, calls=%fused_computation.23 | convolution fusion | flops 1409286144 | bytes 8257536 | tf_op jit(solution)/shard_map/rfc,fkdc->rfkd/dot_general | solution.py:27
  200.6 3.9 fusion
  204.4 0.0 copy-start.7
  204.5 0.0 copy-start.3
  204.5 0.0 copy-start.4
  204.5 3.0 copy.98
  207.5 0.0 reduce-scatter.4.cloned.1.call-update
  207.5 0.0 copy-done.7
  207.5 0.6 dynamic-slice
  208.7 181.7 %all-reduce.5.cloned.1.call-done = (f32[14,4,128,128]{3,2,1,0:T(8,128)}, f32[14,4,128,128]{3,2,1,0:T(8,128)}) async-done(((f32[14,4,128,128]{3,2,1,0:T(8,128)}, f32[14,4,128,128]{3,2,1,0:T(8,128)}), (f32[14,4,128,128]{3,2,1,0:T(8,128)}, f32[14,4,128,128]{3,2,1,0:T(8,128)})) %all-reduce.5.cloned.1.call-update) | async-done | bytes 7340048
  390.5 0.0 copy-done.3
  390.5 0.0 copy-done.4
  390.5 1.8 dynamic-slice_add_fusion
  392.3 36.3 %reduce-scatter.4.cloned.1.call-done = f32[128,512]{1,0:T(8,128)} async-done(((f32[128,4096]{1,0:T(8,128)}), f32[128,512]{1,0:T(8,128)}) %reduce-scatter.4.cloned.1.call-update) | async-done | bytes 262160 | tf_op jit(solution)/shard_map/reduce_scatter | solution.py:35
  (6 shorter events, 0.0 us)
Async XLA Ops:
  7.2 86.3 %all-gather.5.cloned.1.call-start = ((), (), s32[]{:S(2)}) async-start(), calls=%async_computation.2 | async-start | bytes 3784704 | tf_op jit(solution)/shard_map/all_gather | solution.py:13
  8.8 165.2 %all-gather.3.cloned.1.call-start = ((), (), s32[]{:S(2)}) async-start(), calls=%async_computation.1 | async-start | bytes 3784704 | tf_op jit(solution)/shard_map/all_gather | solution.py:14
  10.5 5.0 %copy-start.6 = (s32[14,4]{0,1:T(4,128)S(1)}, s32[14,4]{0,1:T(4,128)}, u32[]{:S(2)}) copy-start(s32[14,4]{0,1:T(4,128)} %param.15) | copy-start | bytes 676
  10.5 380.0 %all-reduce.5.cloned.1.call-start = ((), (), s32[]{:S(2)}) async-start(), calls=%async_computation.4 | async-start | bytes 14680064
  18.3 5.4 %copy-start.2 = (f32[128,4096]{1,0:T(8,128)S(1)}, f32[128,4096]{1,0:T(8,128)}, u32[]{:S(2)}) copy-start(f32[128,4096]{1,0:T(8,128)} %param.10) | copy-start | bytes 6291460
  23.7 3.9 copy-start.5
  93.5 9.7 %copy-start = (f32[14,4,128,128]{2,3,1,0:T(8,128)S(1)}, f32[14,4,128,128]{2,3,1,0:T(8,128)}, u32[]{:S(2)}) copy-start(f32[14,4,128,128]{2,3,1,0:T(8,128)} %copy.50) | copy-start | bytes 11010052
  174.0 9.8 %copy-start.1 = (f32[14,4,128,128]{2,3,1,0:T(8,128)S(1)}, f32[14,4,128,128]{2,3,1,0:T(8,128)}, u32[]{:S(2)}) copy-start(f32[14,4,128,128]{2,3,1,0:T(8,128)} %copy.58) | copy-start | bytes 11010052
  194.3 234.3 %reduce-scatter.4.cloned.1.call-start = ((), (), s32[]{:S(2)}) async-start(), calls=%async_computation.3 | async-start | bytes 2359296 | tf_op jit(solution)/shard_map/reduce_scatter | solution.py:35
  204.4 3.1 copy-start.7
  204.5 186.0 %copy-start.3 = (f32[14,4,4,128]{3,2,1,0:T(4,128)S(1)}, f32[14,4,4,128]{3,2,1,0:T(4,128)}, u32[]{:S(2)}) copy-start(f32[14,4,4,128]{3,2,1,0:T(4,128)} %param.17) | copy-start | bytes 344068
  204.5 186.0 %copy-start.4 = (f32[14,4,4,128]{3,2,1,0:T(4,128)S(1)}, f32[14,4,4,128]{3,2,1,0:T(4,128)}, u32[]{:S(2)}) copy-start(f32[14,4,4,128]{3,2,1,0:T(4,128)} %param.16) | copy-start | bytes 344068
Sparse Core Ops, SparseCore 0:
  11.1 82.2 all-gather.4
  96.6 77.4 all-gather.2
  194.4 196.0 all-reduce.4
  393.5 35.0 reduce-scatter.3
where the time goes:
time: 436 us; the launch traced here: 435 us
  waiting for transfers between devices  341 us (78%)
  matrix products  40 us (9%)
  local copies, waits for them, and re-layouts  36.9 us (8%)
  between operations  14.6 us (3%)
    unnamed x5, waiting for transfers between devices  182 us
    all_gather x1, waiting for transfers between devices, shards(): lax.all_gather(down_blocks, 'tok', axis=2, tiled=True)  65.5 us
    all_gather x1, waiting for transfers between devices, shards(): lax.all_gather(up_blocks, 'tok', axis=2, tiled=True)  57.8 us
    reduce_scatter x1, waiting for transfers between devices, shards(): lax.psum_scatter(partial_value, 'hid', scatter_dimension=1, tiled=True)  36.3 us
    unnamed x22, local copies, waits for them, and re-layouts  11.6 us
    dot_general x1, matrix products, shards(): jnp.einsum('rfkd,fkcd->rfc', cot_sel, down_full, precision=highest)  9.77 us
    dot_general x1, matrix products, shards(): pre_act = jnp.einsum('rfkd,fkdc->rfc', x_sel, up_full, precision=highest)  9.65 us
  transfers between devices with their start and end apart: 4, of which 4 were waited for; matrix products, arithmetic and copies ran while one was open for 13% of the time, Pallas kernels for 0%

commit v1 on v0

--- a/solution.py
+++ b/solution.py
@@ -9,9 +9,18 @@
     row_count = inputs.shape[0]
     block = up_blocks.shape[3]
     block_count = inputs.shape[1] // block
+
+    def connect_ports(t0, net_axis):
+        store = []
+        for _ in range(lax.axis_size(net_axis)):
+            store.append(t0)
+        return jnp.concatenate(
+            lax.all_to_all(jnp.stack(store), axis_name=net_axis, split_axis=0, concat_axis=0), 2
+        )
+
     up_full, down_full = (
         lax.all_gather(up_blocks, "tok", axis=2, tiled=True),
-        lax.all_gather(down_blocks, "tok", axis=2, tiled=True),
+        connect_ports(down_blocks, "tok"),
     )
     grad_scale = (row_count * lax.axis_size("tok")) ** (-0.5)
     x_blocks = inputs.reshape(row_count, block_count, block)

time: 436 us -> 405 us (0.929)
  waiting for transfers between devices: 341 us -> 298 us
  starting transfers between devices: 0.42 us -> 12.2 us
  local copies, waits for them, and re-layouts: 36.9 us -> 41.8 us
    all_to_all x0 -> x1, waiting for transfers between devices: none -> 73.6 us  [connect_ports(): lax.all_to_all(jnp.stack(store), axis_name=net_axis, split_axis=0, concat...]
    all_gather x1 -> x0, waiting for transfers between devices: 65.5 us -> none  [shards(): lax.all_gather(down_blocks, 'tok', axis=2, tiled=True)]
    all_gather x1, waiting for transfers between devices: 57.8 us -> 5.07 us  [shards(): lax.all_gather(up_blocks, 'tok', axis=2, tiled=True)]
    all_to_all x0 -> x1, starting transfers between devices: none -> 11.8 us  [connect_ports(): lax.all_to_all(jnp.stack(store), axis_name=net_axis, split_axis=0, concat...]
    reshape x0 -> x1, local copies, waits for them, and re-layouts: none -> 5.03 us  [connect_ports(): jnp.concatenate(lax.all_to_all(jnp.stack(store), axis_name=net_axis, spli...]
    unnamed x22 -> x27, local copies, waits for them, and re-layouts: 11.6 us -> 8.02 us
    unnamed x5 -> x4, waiting for transfers between devices: 182 us -> 183 us
  transfers between devices with their start and end apart: 4 -> 4, of which waited for: 4 -> 4; matrix products, arithmetic and copies ran while one was open for 13% -> 11% of each run, Pallas kernels for 0% -> 0%
where the time goes in v1:
time: 405 us
  waiting for transfers between devices  298 us (74%)
  local copies, waits for them, and re-layouts  41.8 us (10%)
  matrix products  36.7 us (9%)
  between operations  14.6 us (4%)
  starting transfers between devices  12.2 us (3%)
    unnamed x4, waiting for transfers between devices  183 us
    all_to_all x1, waiting for transfers between devices, connect_ports(): lax.all_to_all(jnp.stack(store), axis_name=net_axis, split_axis=0, concat...  73.6 us
    reduce_scatter x1, waiting for transfers between devices, shards(): lax.psum_scatter(partial_value, 'hid', scatter_dimension=1, tiled=True)  36.4 us
    all_to_all x1, starting transfers between devices, connect_ports(): lax.all_to_all(jnp.stack(store), axis_name=net_axis, split_axis=0, concat...  11.8 us
    dot_general x1, matrix products, shards(): pre_act = jnp.einsum('rfkd,fkdc->rfc', x_sel, up_full, precision=highest)  9.74 us
  transfers between devices with their start and end apart: 4, of which 4 were waited for; matrix products, arithmetic and copies ran while one was open for 11% of the time, Pallas kernels for 0%

profile of v1, /device:TPU:2, one launch (start us, length us, event | category | flops | bytes accessed | tf_op | source)
XLA Modules:
  0.0 404.8 jit_solution(17248044049763401300)
XLA Ops:
  7.2 3.6 stack.2
  10.8 0.0 copy-start.7
  10.8 0.0 copy-start.3
  10.8 11.8 %all-to-all-start = ((f32[32,14,4,4,128]{4,3,2,1,0:T(4,128)}), f32[32,14,4,4,128]{4,3,2,1,0:T(4,128)}, u32[]{:S(2)}, u32[]{:S(2)}) async-start(f32[32,14,4,4,128]{4,3,2,1,0:T(4,128)} %stack.2), calls=%async_computation | async-start | bytes 7340032 | tf_op jit(solution)/shard_map/all_to_all | solution.py:18
  22.6 0.0 all-gather.2.cloned.1.call-start
  22.7 0.0 copy-done.7
  22.7 0.7 copy.58
  23.3 0.0 all-gather.2.cloned.1.call-update
  23.4 0.0 copy-start.9
  23.4 0.0 all-reduce.5.cloned.1.call-start
  23.4 0.0 copy-done.3
  23.4 1.9 copy.47
  25.4 1.9 copy.49
  27.3 0.0 copy-done.9
  27.3 0.1 copy.48
  27.4 0.1 reshape.54
  27.5 2.6 gather_fusion
  30.1 0.0 copy-start.4
  30.1 5.3 %copy.50 = f32[14,4,128,128]{2,3,1,0:T(8,128)} copy(f32[14,4,128,128]{3,2,1,0:T(8,128)} %bitcast.79) | data formatting | bytes 7340032 | tf_op jit(solution)/shard_map/jit(_take)/gather | solution.py:29
  35.4 0.1 copy.46
  35.5 0.0 copy-done.4
  35.5 0.0 copy-start.8
  35.5 1.8 copy.54
  37.3 1.9 copy.56
  39.2 0.0 copy-done.8
  39.2 0.1 copy.55
  39.3 0.1 reshape.58
  39.4 2.6 gather_fusion.1
  42.1 5.1 %copy.57 = f32[14,4,128,128]{2,3,1,0:T(8,128)} copy(f32[14,4,128,128]{3,2,1,0:T(8,128)} %bitcast.80) | data formatting | bytes 7340032 | tf_op jit(solution)/shard_map/jit(_take)/gather | solution.py:28
  47.2 0.1 copy.53
  47.3 73.6 %all-to-all-done = f32[32,14,4,4,128]{4,3,2,1,0:T(4,128)} async-done(((f32[32,14,4,4,128]{4,3,2,1,0:T(4,128)}), f32[32,14,4,4,128]{4,3,2,1,0:T(4,128)}, u32[]{:S(2)}, u32[]{:S(2)}) %all-to-all-start) | async-done | bytes 3670048 | tf_op jit(solution)/shard_map/all_to_all | solution.py:18
  120.9 5.0 %copy.51 = f32[14,4,32,4,128]{4,3,2,1,0:T(4,128)} copy(f32[14,4,32,4,128]{4,3,1,0,2:T(4,128)} %bitcast.4) | data formatting | bytes 7340032 | tf_op jit(solution)/shard_map/reshape | solution.py:17
  125.9 5.1 %all-gather.2.cloned.1.call-done = f32[14,4,128,128]{3,1,0,2:T(4,128)} async-done(((f32[14,4,4,128]{3,1,0,2:T(4,128)}), f32[14,4,128,128]{3,1,0,2:T(4,128)}) %all-gather.2.cloned.1.call-update) | async-done | bytes 3670032 | tf_op jit(solution)/shard_map/all_gather | solution.py:22
  131.0 0.0 copy-start
  131.0 9.7 %fusion.36 = f32[128,14,128]{2,0,1:T(8,128)S(1)} fusion(f32[14,4,128,128]{3,1,0,2:T(4,128)} %all-gather.2.cloned.1.call-done, f32[14,4,128,128]{2,3,1,0:T(8,128)} %copy.57, pred[14,4]{1,0:T(8,128)(4,1)S(1)} %copy.53), kind=kOutput, calls=%fused_computation.32 | convolution fusion | flops 1410203648 | bytes 8257592 | tf_op jit(solution)/shard_map/rfkd,fkdc->rfc/dot_general | solution.py:30
  140.7 0.0 copy-done
  140.7 0.0 copy-start.2
  140.8 5.5 %multiply_bitcast_fusion = f32[14,4,128,128]{2,3,1,0:T(8,128)} fusion(f32[14,4,128,128]{2,3,1,0:T(8,128)S(1)} %copy-done, pred[14,4]{1,0:T(8,128)(4,1)S(1)} %copy.46, f32[128,14,128]{2,0,1:T(8,128)S(1)} %fusion.36), kind=kOutput, calls=%fused_computation.12 | convolution fusion | flops 1412038656 | bytes 8257592 | tf_op jit(solution)/shard_map/rfc,rfkd->fkcd/dot_general | solution.py:35
  146.2 0.0 copy-done.2
  146.2 0.0 copy-start.1
  146.2 6.3 %fusion.47 = f32[128,14,128,1]{2,0,3,1:T(8,128)S(1)} fusion(f32[14,4,128,128]{3,2,1,0:T(8,128)S(1)} %bitcast.78, f32[14,4,128,128]{2,3,1,0:T(8,128)S(1)} %copy-done, pred[14,4]{1,0:T(8,128)(4,1)S(1)} %copy.46, f32[128,14,128]{2,0,1:T(8,128)S(1)} %fusion.36), kind=kOutput, calls=%fused_computation.35 | convolution fusion | flops 1412038656 | bytes 9175096 | tf_op jit(solution)/shard_map/rfkd,fkcd->rfc/dot_general | solution.py:33
  152.6 0.0 copy-done.1
  152.6 5.3 %fusion.19 = f32[14,4,128,128]{3,2,1,0:T(8,128)} fusion(f32[128,14,128,1]{2,0,3,1:T(8,128)S(1)} %fusion.47, f32[14,4,128,128]{2,3,1,0:T(8,128)S(1)} %copy-done.1, pred[14,4]{1,0:T(8,128)(4,1)S(1)} %copy.53), kind=kOutput, calls=%fused_computation.21 | convolution fusion | flops 1411121152 | bytes 8257592 | tf_op jit(solution)/shard_map/rfkd,rfc->fkdc/dot_general | solution.py:43
  157.9 5.1 %copy.63 = f32[14,4,128,128]{3,2,1,0:T(8,128)} copy(f32[14,4,128,128]{2,3,1,0:T(8,128)} %multiply_bitcast_fusion) | data formatting | bytes 7340032 | tf_op jit(solution)/shard_map/mul | solution.py:35
  163.0 0.0 all-reduce.5.cloned.1.call-update
  163.0 0.3 reduce-scatter.4.cloned.1.call-start
  163.3 6.0 %fusion.22 = f32[128,14,4,128]{3,0,2,1:T(8,128)S(1)} fusion(f32[128,14,128,1]{2,0,3,1:T(8,128)S(1)} %fusion.47, f32[14,4,128,128]{3,1,0,2:T(4,128)} %all-gather.2.cloned.1.call-done), kind=kOutput, calls=%fused_computation.22 | convolution fusion | flops 1409286144 | bytes 8257536 | tf_op jit(solution)/shard_map/rfc,fkdc->rfkd/dot_general | solution.py:36
  169.3 3.9 fusion
  173.2 0.0 copy-start.10
  173.2 0.0 copy-start.5
  173.2 0.0 copy-start.6
  173.2 3.0 copy.87
  176.2 0.0 reduce-scatter.4.cloned.1.call-update
  176.2 0.0 copy-done.10
  176.2 0.6 dynamic-slice
  177.5 182.5 %all-reduce.5.cloned.1.call-done = (f32[14,4,128,128]{3,2,1,0:T(8,128)}, f32[14,4,128,128]{3,2,1,0:T(8,128)}) async-done(((f32[14,4,128,128]{3,2,1,0:T(8,128)}, f32[14,4,128,128]{3,2,1,0:T(8,128)}), (f32[14,4,128,128]{3,2,1,0:T(8,128)}, f32[14,4,128,128]{3,2,1,0:T(8,128)})) %all-reduce.5.cloned.1.call-update) | async-done | bytes 7340048
  360.0 0.0 copy-done.5
  360.0 0.0 copy-done.6
  360.0 1.8 dynamic-slice_add_fusion
  361.8 36.4 %reduce-scatter.4.cloned.1.call-done = f32[128,512]{1,0:T(8,128)} async-done(((f32[128,4096]{1,0:T(8,128)}), f32[128,512]{1,0:T(8,128)}) %reduce-scatter.4.cloned.1.call-update) | async-done | bytes 262160 | tf_op jit(solution)/shard_map/reduce_scatter | solution.py:44
  (6 shorter events, 0.0 us)
Async XLA Ops:
  10.8 11.9 %copy-start.7 = (f32[14,4,4,128]{3,2,1,0:T(4,128)S(1)}, f32[14,4,4,128]{3,2,1,0:T(4,128)}, u32[]{:S(2)}) copy-start(f32[14,4,4,128]{3,2,1,0:T(4,128)} %param.12) | copy-start | bytes 344068
  10.8 12.6 %copy-start.3 = (f32[128,4096]{1,0:T(8,128)S(1)}, f32[128,4096]{1,0:T(8,128)}, u32[]{:S(2)}) copy-start(f32[128,4096]{1,0:T(8,128)} %param.11) | copy-start | bytes 6291460
  10.8 110.1 %all-to-all-start = ((f32[32,14,4,4,128]{4,3,2,1,0:T(4,128)}), f32[32,14,4,4,128]{4,3,2,1,0:T(4,128)}, u32[]{:S(2)}, u32[]{:S(2)}) async-start(f32[32,14,4,4,128]{4,3,2,1,0:T(4,128)} %stack.2), calls=%async_computation | async-start | bytes 7340032 | tf_op jit(solution)/shard_map/all_to_all | solution.py:18
  22.6 108.4 %all-gather.2.cloned.1.call-start = ((), (), s32[]{:S(2)}) async-start(), calls=%async_computation.2 | async-start | bytes 3784704 | tf_op jit(solution)/shard_map/all_gather | solution.py:22
  23.4 3.9 copy-start.9
  23.4 336.6 %all-reduce.5.cloned.1.call-start = ((), (), s32[]{:S(2)}) async-start(), calls=%async_computation.4 | async-start | bytes 14680064
  30.1 5.4 %copy-start.4 = (f32[128,4096]{1,0:T(8,128)S(1)}, f32[128,4096]{1,0:T(8,128)}, u32[]{:S(2)}) copy-start(f32[128,4096]{1,0:T(8,128)} %param.10) | copy-start | bytes 6291460
  35.5 3.7 copy-start.8
  131.0 9.8 %copy-start = (f32[14,4,128,128]{2,3,1,0:T(8,128)S(1)}, f32[14,4,128,128]{2,3,1,0:T(8,128)}, u32[]{:S(2)}) copy-start(f32[14,4,128,128]{2,3,1,0:T(8,128)} %copy.50) | copy-start | bytes 11010052
  140.7 5.5 %copy-start.2 = (f32[14,4,32,4,128]{4,3,2,1,0:T(4,128)S(1)}, f32[14,4,32,4,128]{4,3,2,1,0:T(4,128)}, u32[]{:S(2)}) copy-start(f32[14,4,32,4,128]{4,3,2,1,0:T(4,128)} %copy.51) | copy-start | bytes 11010052
  146.2 6.3 %copy-start.1 = (f32[14,4,128,128]{2,3,1,0:T(8,128)S(1)}, f32[14,4,128,128]{2,3,1,0:T(8,128)}, u32[]{:S(2)}) copy-start(f32[14,4,128,128]{2,3,1,0:T(8,128)} %copy.57) | copy-start | bytes 11010052
  163.0 235.2 %reduce-scatter.4.cloned.1.call-start = ((), (), s32[]{:S(2)}) async-start(), calls=%async_computation.3 | async-start | bytes 2359296 | tf_op jit(solution)/shard_map/reduce_scatter | solution.py:44
  173.2 3.1 copy-start.10
  173.2 186.8 %copy-start.5 = (f32[14,4,4,128]{3,2,1,0:T(4,128)S(1)}, f32[14,4,4,128]{3,2,1,0:T(4,128)}, u32[]{:S(2)}) copy-start(f32[14,4,4,128]{3,2,1,0:T(4,128)} %param.17) | copy-start | bytes 344068
  173.2 186.8 %copy-start.6 = (f32[14,4,4,128]{3,2,1,0:T(4,128)S(1)}, f32[14,4,4,128]{3,2,1,0:T(4,128)}, u32[]{:S(2)}) copy-start(f32[14,4,4,128]{3,2,1,0:T(4,128)} %param.16) | copy-start | bytes 344068
Sparse Core Ops, SparseCore 0:
  26.6 104.3 all-gather.1
  163.1 196.7 all-reduce.4
  363.1 35.0 reduce-scatter.3
